TPU v7x, 32 devices: a whole 2x2x4 slice. The times are simulated.
32 devices in a mesh: lon: 8 (over y, x, core), spec: 4 (over z).
Axes of the slice: x: 2, y: 2, z: 4, core: 2. Of those that a mesh axis runs over, the one named last changes fastest.
Arguments:
- lam_final: float32 [1296, 64, 1024], P('spec', None, 'lon'), may hold values from -6 to 6
- stored_source: bfloat16 [2, 1296, 64, 1024], P(None, 'spec', None, 'lon'), may hold values from 0.19921875 to 1.1953125
- mixing: bfloat16 [1296, 1296], replicated, may hold values from -0.15625 to 0.15625
- drift_x: float32 [1296], replicated, may hold values from -0.45 to 0.45
- drift_y: float32 [1296], replicated, may hold values from -0.45 to 0.45
- ocean_mask: int32 [64, 1024], P(None, 'lon'), may hold values 0 or 1
- misfit: float32 [2, 64, 1024], P(None, None, 'lon'), may hold values from -6 to 6
- obs_mask: int32 [2, 64, 1024], P(None, None, 'lon'), may hold values 0 or 1
Outputs:
- lam_start: float32 [1296, 64, 1024], P('spec', None, 'lon')
All inputs are finite; a program needn't handle non-finite values. No bound on the sum of `ocean_mask` or of `obs_mask` on one device may be relied on, other than what follows from the above.
Results may differ from a plain program's by a relative error of at most 0.0028.
Values may be sent and summed in bfloat16 or wider, within the bound.
A program may use at most 192 MiB of HBM per device.

v0:
```python
import jax
import jax.numpy as jnp
from jax import lax
from jax.sharding import PartitionSpec as P

STEPS = 2


def with_halo(block, sides, width):
    for axis, dim in sides:
        count = lax.axis_size(axis)
        forward = [(i, i + 1) for i in range(count - 1)]
        forward.append((count - 1, 0))
        backward = [(target, source) for source, target in forward]
        low = lax.ppermute(
            lax.slice_in_dim(block, block.shape[dim] - width, None, axis=dim), axis, forward
        )
        high = lax.ppermute(lax.slice_in_dim(block, 0, width, axis=dim), axis, backward)
        block = jnp.concatenate([low, block, high], axis=dim)
    return block


def couple_local(rounded, mixing):
    flat = rounded.reshape(rounded.shape[0], -1)
    coupled = lax.dot_general(
        mixing, flat, (((0,), (0,)), ((), ())), preferred_element_type=jnp.float32
    )
    return coupled.astype(jnp.bfloat16).reshape(rounded.shape)


def advect_step(adjoint, speed_x, speed_y, northern, southern):
    padded = with_halo(adjoint, (("lon", 2),), 1)
    eastern = padded[:, :, 2:]
    western = padded[:, :, :-2]
    speed_x = speed_x[:, None, None]
    speed_y = speed_y[:, None, None]
    stay = 1.0 - jnp.abs(speed_x) - jnp.abs(speed_y)
    result = (
        stay * adjoint + jnp.maximum(speed_x, 0.0) * eastern + jnp.maximum(-speed_x, 0.0) * western
    )
    return result + jnp.maximum(speed_y, 0.0) * northern + jnp.maximum(-speed_y, 0.0) * southern


def per_device(lam_final, stored_source, mixing, drift_x, drift_y, ocean_mask, misfit, obs_mask):
    spec_index = lax.axis_index("spec")
    own_count = lam_final.shape[0]
    speed_x = lax.dynamic_slice_in_dim(drift_x, spec_index * own_count, own_count)
    speed_y = lax.dynamic_slice_in_dim(drift_y, spec_index * own_count, own_count)
    ocean_field = ocean_mask.astype(jnp.float32)[None]
    adjoint = lam_final
    for step_index in reversed(range(STEPS)):
        forcing = misfit[step_index] * obs_mask[step_index].astype(jnp.float32)
        adjoint = (adjoint + forcing[None]) * ocean_field
        rounded = adjoint.astype(jnp.bfloat16)
        coupled = couple_local(
            lax.all_to_all(rounded, "spec", split_axis=1, concat_axis=0, tiled=True), mixing
        )
        coupled = lax.all_to_all(coupled, "spec", split_axis=0, concat_axis=1, tiled=True)
        adjoint = adjoint + stored_source[step_index].astype(jnp.float32) * coupled.astype(
            jnp.float32
        )
        zero_row = jnp.zeros_like(adjoint[:, :1])
        northern = jnp.concatenate([adjoint[:, 1:], zero_row], axis=1)
        southern = jnp.concatenate([zero_row, adjoint[:, :-1]], axis=1)
        adjoint = advect_step(adjoint, speed_x, speed_y, northern, southern)
    return adjoint


def solution(mesh):
    in_specs = (
        P("spec", None, "lon"),
        P(None, "spec", None, "lon"),
        P(),
        P(),
        P(),
        P(None, "lon"),
        P(None, None, "lon"),
        P(None, None, "lon"),
    )
    out_specs = P("spec", None, "lon")
    return jax.shard_map(
        per_device, mesh=mesh, in_specs=in_specs, out_specs=out_specs, check_vma=False
    )
```

profile of v0, /device:TPU:0, one launch (start us, length us, event | category | flops | bytes accessed | tf_op | source)
XLA Modules:
  0.0 733.8 jit_solution(17673067778883216311)
XLA Ops:
  1.6 11.5 %fusion.17 = bf16[324,64,128]{2,0,1:T(8,128)(2,1)S(1)} fusion(f32[324,64,128]{2,1,0:T(8,128)} %param.8, f32[64,128]{1,0:T(8,128)S(1)} %convert_element_type.66, f32[64,128]{1,0:T(8,128)S(1)} %get-tuple-element.17), kind=kLoop, calls=%fused_computation.24 | loop fusion | flops 7962624 | bytes 15990784 | tf_op jit(solution)/shard_map/convert_element_type | solution.py:54
  13.1 125.0 %all_to_all.48 = bf16[324,64,128]{2,0,1:T(8,128)(2,1)S(1)} all-to-all(bf16[324,64,128]{2,0,1:T(8,128)(2,1)S(1)} %fusion.17), channel_id=1, replica_groups=mesh['lon'=8,'spec'=4] {'spec'}, dimensions={1} | all-to-all | bytes 10616832 | tf_op jit(solution)/shard_map/all_to_all | solution.py:56
  138.9 9.2 %fusion.22 = bf16[162,8,16,128]{3,1,2,0:T(8,128)(2,1)S(1)} fusion(bf16[1296,1296]{1,0:T(8,128)(2,1)S(1)} %copy-done.2, bf16[162,8,16,128]{3,2,1,0:T(8,128)(2,1)S(1)} %bitcast.67), kind=kOutput, calls=%fused_computation.33 | convolution fusion | flops 6882361344 | bytes 13976064 | tf_op jit(solution)/shard_map/dot_general | solution.py:25
  158.4 10.6 %fusion.34 = (bf16[1,324,64,128]{3,2,1,0:T(8,128)(2,1)}, bf16[1,324,64,128]{3,2,1,0:T(8,128)(2,1)}) fusion(bf16[2,324,64,128]{3,2,1,0:T(8,128)(2,1)} %param.9), kind=kLoop, calls=%fused_computation.47 | loop fusion | bytes 21233664 | tf_op jit(solution)/shard_map/slice | solution.py:59
  169.0 104.8 %all-to-all-done.1 = bf16[1296,16,128]{2,1,0:T(8,128)(2,1)} async-done(((bf16[1296,16,128]{2,1,0:T(8,128)(2,1)}), bf16[1296,16,128]{2,1,0:T(8,128)(2,1)}, u32[]{:S(2)}, u32[]{:S(2)}) %all-to-all-start.1) | async-done | bytes 5308448 | tf_op jit(solution)/shard_map/all_to_all | solution.py:58
  277.6 12.9 %fusion.15 = f32[324,64,128]{2,0,1:T(8,128)S(1)} fusion(f32[4,324,16,128]{3,1,2,0:T(8,128)S(1)} %copy.18, f32[324,64,128]{2,1,0:T(8,128)} %param.8, bf16[1,324,64,128]{3,2,1,0:T(8,128)(2,1)S(1)} %bitcast.63, f32[64,128]{1,0:T(8,128)S(1)} %convert_element_type.66, f32[64,128]{1,0:T(8,128)S(1)} %get-tuple-element.17), kind=kLoop, calls=%fused_computation.21 | loop fusion | flops 13271040 | bytes 37224448 | tf_op jit(solution)/shard_map/add | solution.py:59
  290.5 9.5 %fusion.32 = (f32[324,64,1]{2,0,1:T(8,128)}, f32[324,64,1]{2,0,1:T(8,128)}) fusion(f32[324,64,128]{2,0,1:T(8,128)S(1)} %fusion.15), kind=kLoop, calls=%fused_computation.45 | loop fusion | bytes 331776 | tf_op jit(solution)/shard_map/slice | solution.py:18
  301.1 6.5 copy.19
  307.6 6.5 copy.21
  317.1 15.7 %fusion.33 = (f32[324,63,128]{2,0,1:T(8,128)}, f32[324,63,128]{2,0,1:T(8,128)}) fusion(f32[324,64,128]{2,0,1:T(8,128)} %copy-done), kind=kLoop, calls=%fused_computation.46 | loop fusion | bytes 41803776 | tf_op jit(solution)/shard_map/slice | solution.py:63
  338.4 5.6 copy.22
  344.0 30.8 %fusion.28 = (bf16[324,64,128]{2,0,1:T(8,128)(2,1)S(1)}, f32[324,64,128]{2,0,1:T(8,128)}) fusion(f32[64,128]{1,0:T(8,128)S(1)} %convert_element_type.66, f32[64,128]{1,0:T(8,128)S(1)} %get-tuple-element.18, f32[324,63,128]{2,0,1:T(8,128)} %get-tuple-element.14, f32[324]{0:T(512)S(1)} %get-tuple-element.23, f32[324,63,128]{2,0,1:T(8,128)} %get-tuple-element.13, ...), kind=kLoop, calls=%fused_computation.42 | loop fusion | flops 37158912 | bytes 47681872 | tf_op jit(solution)/shard_map/convert_element_type | solution.py:54
  374.8 121.0 %all_to_all.49 = bf16[324,64,128]{2,0,1:T(8,128)(2,1)S(1)} all-to-all(bf16[324,64,128]{2,0,1:T(8,128)(2,1)S(1)} %get-tuple-element.5), channel_id=1, replica_groups=mesh['lon'=8,'spec'=4] {'spec'}, dimensions={1} | all-to-all | bytes 10616832 | tf_op jit(solution)/shard_map/all_to_all | solution.py:56
  496.6 9.5 %fusion.25 = bf16[162,8,16,128]{3,1,2,0:T(8,128)(2,1)S(1)} fusion(bf16[1296,1296]{1,0:T(8,128)(2,1)S(1)} %copy-done.3, bf16[162,8,16,128]{3,2,1,0:T(8,128)(2,1)S(1)} %bitcast.68), kind=kOutput, calls=%fused_computation.34 | convolution fusion | flops 6882361344 | bytes 13976064 | tf_op jit(solution)/shard_map/dot_general | solution.py:25
  507.9 119.2 %all_to_all.50 = bf16[1296,16,128]{2,1,0:T(8,128)(2,1)S(1)} all-to-all(bf16[1296,16,128]{2,1,0:T(8,128)(2,1)S(1)} %bitcast.65), channel_id=1, replica_groups=mesh['lon'=8,'spec'=4] {'spec'}, dimensions={0} | all-to-all | bytes 10616832 | tf_op jit(solution)/shard_map/all_to_all | solution.py:58
  632.2 8.3 %fusion.14 = f32[324,64,128]{2,0,1:T(8,128)S(1)} fusion(f32[324,64,128]{2,0,1:T(8,128)S(1)} %bitcast.59, f32[4,324,16,128]{3,1,2,0:T(8,128)} %copy.25, bf16[1,324,64,128]{3,2,1,0:T(8,128)(2,1)} %get-tuple-element.15), kind=kLoop, calls=%fused_computation.19 | loop fusion | flops 7962624 | bytes 37158912 | tf_op jit(solution)/shard_map/add | solution.py:59
  640.5 9.4 %fusion.31 = (f32[324,64,1]{2,0,1:T(8,128)}, f32[324,64,1]{2,0,1:T(8,128)}) fusion(f32[324,64,128]{2,0,1:T(8,128)S(1)} %fusion.14), kind=kLoop, calls=%fused_computation.44 | loop fusion | bytes 331776 | tf_op jit(solution)/shard_map/slice | solution.py:18
  650.9 6.5 copy.26
  657.4 6.5 copy.28
  666.6 15.7 %fusion.30 = (f32[324,63,128]{2,0,1:T(8,128)}, f32[324,63,128]{2,0,1:T(8,128)}) fusion(f32[324,64,128]{2,0,1:T(8,128)} %copy-done.1), kind=kLoop, calls=%fused_computation.43 | loop fusion | bytes 41803776 | tf_op jit(solution)/shard_map/slice | solution.py:63
  682.3 5.6 copy.27
  687.8 5.6 copy.29
  693.5 29.9 %fusion.3 = f32[324,64,128]{2,0,1:T(8,128)} fusion(f32[324,64,128]{2,0,1:T(8,128)} %copy-done.1, f32[324,64,1]{2,0,1:T(8,128)} %copy.29, f32[324,64,1]{2,0,1:T(8,128)} %copy.27, f32[324,63,128]{2,0,1:T(8,128)} %get-tuple-element.8, f32[324,63,128]{2,0,1:T(8,128)} %get-tuple-element.7, f32[324]{0:T(512)S(1)} %get-tuple-element.23, ...), kind=kLoop, calls=%fused_computation.4 | loop fusion | flops 29196288 | bytes 42307920 | tf_op jit(solution)/shard_map/add | solution.py:41
  723.4 10.2 %copy.30 = f32[324,64,128]{2,1,0:T(8,128)} copy(f32[324,64,128]{2,0,1:T(8,128)} %fusion.3) | data formatting | bytes 21233664 | tf_op jit(solution)/shard_map/add | solution.py:41
  (39 shorter events, 37.3 us)
Async XLA Ops:
  13.1 125.8 %copy-start.2 = (bf16[1296,1296]{1,0:T(8,128)(2,1)S(1)}, bf16[1296,1296]{1,0:T(8,128)(2,1)}, u32[]{:S(2)}) copy-start(bf16[1296,1296]{1,0:T(8,128)(2,1)} %param.10) | copy-start | bytes 10077700
  152.3 121.5 %all-to-all-start.1 = ((bf16[1296,16,128]{2,1,0:T(8,128)(2,1)}), bf16[1296,16,128]{2,1,0:T(8,128)(2,1)}, u32[]{:S(2)}, u32[]{:S(2)}) async-start(bf16[1296,16,128]{2,1,0:T(8,128)(2,1)} %bitcast.64), calls=%async_computation.1 | async-start | bytes 10616832 | tf_op jit(solution)/shard_map/all_to_all | solution.py:58
  169.0 108.5 %slice-start.3 = ((s8[5308416]{0:T(1024)(128)(4,1)}), s8[1114112]{0:T(1024)(128)(4,1)S(1)}, s32[]{:S(2)}) async-start(s8[5308416]{0:T(1024)(128)(4,1)} %bitcast.62), calls=%async_computation.7 | async-start | bytes 2228224
  273.8 3.8 slice-start.4
  290.5 10.6 %copy-start = (f32[324,64,128]{2,0,1:T(8,128)}, f32[324,64,128]{2,0,1:T(8,128)S(1)}, u32[]{:S(2)}) copy-start(f32[324,64,128]{2,0,1:T(8,128)S(1)} %fusion.15) | copy-start | bytes 31850500
  314.0 24.4 %collective-permute-start.1 = (f32[324,64,1]{0,1,2:T(8,128)S(1)}, f32[324,64,1]{0,1,2:T(8,128)S(1)}, u32[]{:S(2)}, u32[]{:S(2)}) collective-permute-start(f32[324,64,1]{0,1,2:T(8,128)S(1)} %copy.21), channel_id=1, source_target_pairs={{0,4},{4,8},{8,12},{12,16},{16,20},{20,24},{24,28},{28,0},{1,5},{5... | collective-permute-start | bytes 248840 | tf_op jit(solution)/shard_map/ppermute | solution.py:15
  314.1 18.7 %collective-permute-start = (f32[324,64,1]{0,1,2:T(8,128)S(1)}, f32[324,64,1]{0,1,2:T(8,128)S(1)}, u32[]{:S(2)}, u32[]{:S(2)}) collective-permute-start(f32[324,64,1]{0,1,2:T(8,128)S(1)} %copy.19), channel_id=1, source_target_pairs={{4,0},{8,4},{12,8},{16,12},{20,16},{24,20},{28,24},{0,28},{5,1},{9... | collective-permute-start | bytes 248840 | tf_op jit(solution)/shard_map/ppermute | solution.py:18
  374.8 121.8 %copy-start.3 = (bf16[1296,1296]{1,0:T(8,128)(2,1)S(1)}, bf16[1296,1296]{1,0:T(8,128)(2,1)}, u32[]{:S(2)}) copy-start(bf16[1296,1296]{1,0:T(8,128)(2,1)} %param.10) | copy-start | bytes 10077700
  507.9 124.2 %slice-start = ((s8[10747904]{0:T(1024)(128)(4,1)}), s8[4194304]{0:T(1024)(128)(4,1)S(1)}, s32[]{:S(2)}) async-start(s8[10747904]{0:T(1024)(128)(4,1)} %bitcast.58), calls=%async_computation.4 | async-start | bytes 8388608
  507.9 124.2 %slice-start.1 = ((s8[10747904]{0:T(1024)(128)(4,1)}), s8[4194304]{0:T(1024)(128)(4,1)S(1)}, s32[]{:S(2)}) async-start(s8[10747904]{0:T(1024)(128)(4,1)} %bitcast.58), calls=%async_computation.5 | async-start | bytes 8388608
  627.2 5.0 slice-start.2
  640.5 10.4 %copy-start.1 = (f32[324,64,128]{2,0,1:T(8,128)}, f32[324,64,128]{2,0,1:T(8,128)S(1)}, u32[]{:S(2)}) copy-start(f32[324,64,128]{2,0,1:T(8,128)S(1)} %fusion.14) | copy-start | bytes 31850500
  663.9 23.9 %collective-permute-start.3 = (f32[324,64,1]{0,1,2:T(8,128)S(1)}, f32[324,64,1]{0,1,2:T(8,128)S(1)}, u32[]{:S(2)}, u32[]{:S(2)}) collective-permute-start(f32[324,64,1]{0,1,2:T(8,128)S(1)} %copy.28), channel_id=1, source_target_pairs={{0,4},{4,8},{8,12},{12,16},{16,20},{20,24},{24,28},{28,0},{1,5},{5... | collective-permute-start | bytes 248840 | tf_op jit(solution)/shard_map/ppermute | solution.py:15
  664.0 18.3 %collective-permute-start.2 = (f32[324,64,1]{0,1,2:T(8,128)S(1)}, f32[324,64,1]{0,1,2:T(8,128)S(1)}, u32[]{:S(2)}, u32[]{:S(2)}) collective-permute-start(f32[324,64,1]{0,1,2:T(8,128)S(1)} %copy.26), channel_id=1, source_target_pairs={{4,0},{8,4},{12,8},{16,12},{20,16},{24,20},{28,24},{0,28},{5,1},{9... | collective-permute-start | bytes 248840 | tf_op jit(solution)/shard_map/ppermute | solution.py:18
where the time goes:
time: 740 us; the launch traced here: 734 us
  blocking collectives  365 us (49%)
  local copies, waits for them, and re-layouts  138 us (19%)
  waiting for transfers between devices  105 us (14%)
  other arithmetic  95.9 us (13%)
  matrix products  18.7 us (3%)
  starting transfers between devices  11 us (1%)
    all_to_all x2, blocking collectives, per_device(): lax.all_to_all(rounded, 'spec', split_axis=1, concat_axis=0, tiled=True)  246 us
    all_to_all x1, blocking collectives, per_device(): lax.all_to_all(coupled, 'spec', split_axis=0, concat_axis=1, tiled=True)  119 us
    all_to_all x1, waiting for transfers between devices, per_device(): lax.all_to_all(coupled, 'spec', split_axis=0, concat_axis=1, tiled=True)  105 us
    convert_element_type x2, other arithmetic, per_device(): rounded = adjoint.astype(jnp.bfloat16)  42.3 us
    slice x4, local copies, waits for them, and re-layouts, with_halo(): lax.slice_in_dim(block, 0, width, axis=dim)  31.8 us
    slice x2, local copies, waits for them, and re-layouts, per_device(): northern = jnp.concatenate([adjoint[:, 1:], zero_row], axis=1)  31.4 us
    add x1, other arithmetic, advect_step(): result + jnp.maximum(speed_y, 0.0) * northern  29.9 us
    add x2, other arithmetic, per_device(): adjoint + stored_source[step_index].astype(jnp.float32) * coupled.astype(...  21.3 us
  transfers between devices with their start and end apart: 5, of which 1 were waited for; matrix products, arithmetic and copies ran while one was open for 7% of the time, Pallas kernels for 0%

commit v1 on v0

--- a/solution.py
+++ b/solution.py
@@ -55,7 +55,12 @@
         coupled = couple_local(
             lax.all_to_all(rounded, "spec", split_axis=1, concat_axis=0, tiled=True), mixing
         )
-        coupled = lax.all_to_all(coupled, "spec", split_axis=0, concat_axis=1, tiled=True)
+        coupled = jnp.concatenate(
+            lax.all_to_all(
+                jnp.stack(jnp.split(coupled, lax.axis_size("spec"), axis=0)), "spec", 0, 0
+            ),
+            axis=1,
+        )
         adjoint = adjoint + stored_source[step_index].astype(jnp.float32) * coupled.astype(
             jnp.float32
         )

time: 740 us -> 772 us (1.043)
  other arithmetic: 95.9 us -> 116 us
  local copies, waits for them, and re-layouts: 138 us -> 150 us
    convert_element_type x0 -> x2, other arithmetic: none -> 13.8 us  [per_device(): coupled.astype(jnp.float32)]
    convert_element_type x2, local copies, waits for them, and re-layouts: 8.65 us -> 18.6 us  [per_device(): coupled.astype(jnp.float32)]
where the time goes in v1:
time: 772 us; the launch traced here: 765 us
  blocking collectives  365 us (47%)
  local copies, waits for them, and re-layouts  150 us (19%)
  other arithmetic  116 us (15%)
  waiting for transfers between devices  105 us (14%)
  matrix products  18.7 us (2%)
  starting transfers between devices  10.6 us (1%)
    all_to_all x2, blocking collectives, per_device(): lax.all_to_all(rounded, 'spec', split_axis=1, concat_axis=0, tiled=True)  246 us
    all_to_all x1, blocking collectives, per_device(): lax.all_to_all(jnp.stack(jnp.split(coupled, lax.axis_size('spec'), axis=0...  119 us
    all_to_all x1, waiting for transfers between devices, per_device(): lax.all_to_all(jnp.stack(jnp.split(coupled, lax.axis_size('spec'), axis=0...  105 us
    convert_element_type x2, other arithmetic, per_device(): rounded = adjoint.astype(jnp.bfloat16)  42.3 us
    slice x4, local copies, waits for them, and re-layouts, with_halo(): lax.slice_in_dim(block, 0, width, axis=dim)  32.1 us
    slice x2, local copies, waits for them, and re-layouts, per_device(): northern = jnp.concatenate([adjoint[:, 1:], zero_row], axis=1)  31.6 us
    add x1, other arithmetic, advect_step(): result + jnp.maximum(speed_y, 0.0) * northern  29.9 us
    add x2, other arithmetic, per_device(): adjoint + stored_source[step_index].astype(jnp.float32) * coupled.astype(...  24 us
  transfers between devices with their start and end apart: 5, of which 1 were waited for; matrix products, arithmetic and copies ran while one was open for 7% of the time, Pallas kernels for 0%

profile of v1, /device:TPU:0, one launch (start us, length us, event | category | flops | bytes accessed | tf_op | source)
XLA Modules:
  0.0 765.4 jit_solution(11980220299925466079)
XLA Ops:
  1.6 11.5 %fusion.17 = bf16[324,64,128]{2,0,1:T(8,128)(2,1)S(1)} fusion(f32[324,64,128]{2,1,0:T(8,128)} %param.8, f32[64,128]{1,0:T(8,128)S(1)} %convert_element_type.60, f32[64,128]{1,0:T(8,128)S(1)} %get-tuple-element.25), kind=kLoop, calls=%fused_computation.26 | loop fusion | flops 7962624 | bytes 15990784 | tf_op jit(solution)/shard_map/convert_element_type | solution.py:54
  13.1 125.0 %all_to_all.40 = bf16[324,64,128]{2,0,1:T(8,128)(2,1)S(1)} all-to-all(bf16[324,64,128]{2,0,1:T(8,128)(2,1)S(1)} %fusion.17), channel_id=1, replica_groups=mesh['lon'=8,'spec'=4] {'spec'}, dimensions={1} | all-to-all | bytes 10616832 | tf_op jit(solution)/shard_map/all_to_all | solution.py:56
  138.9 9.2 %fusion.18 = bf16[1296,2048]{1,0:T(8,128)(2,1)S(1)} fusion(bf16[1296,1296]{1,0:T(8,128)(2,1)S(1)} %copy-done.2, bf16[162,8,16,128]{3,2,1,0:T(8,128)(2,1)S(1)} %bitcast.102), kind=kOutput, calls=%fused_computation.29 | convolution fusion | flops 6882361344 | bytes 13976064 | tf_op jit(solution)/shard_map/dot_general | solution.py:25
  160.5 10.6 %fusion.30 = (bf16[1,324,64,128]{3,2,1,0:T(8,128)(2,1)}, bf16[1,324,64,128]{3,2,1,0:T(8,128)(2,1)}) fusion(bf16[2,324,64,128]{3,2,1,0:T(8,128)(2,1)} %param.9), kind=kLoop, calls=%fused_computation.59 | loop fusion | bytes 21233664 | tf_op jit(solution)/shard_map/slice | solution.py:64
  171.1 104.8 %all-to-all-done.1 = bf16[4,324,16,128]{3,2,1,0:T(8,128)(2,1)} async-done(((bf16[4,324,16,128]{3,2,1,0:T(8,128)(2,1)}), bf16[4,324,16,128]{3,2,1,0:T(8,128)(2,1)}, u32[]{:S(2)}, u32[]{:S(2)}) %all-to-all-start.1) | async-done | bytes 5308448 | tf_op jit(solution)/shard_map/all_to_all | solution.py:59
  275.9 7.5 convert_bitcast_fusion.1
  283.5 7.3 copy.18
  290.7 16.0 %fusion.15 = f32[324,64,128]{2,0,1:T(8,128)S(1)} fusion(f32[324,4,16,128]{3,0,2,1:T(8,128)S(1)} %copy.18, f32[324,64,128]{2,1,0:T(8,128)} %param.8, bf16[1,324,64,128]{3,2,1,0:T(8,128)(2,1)} %get-tuple-element.16, f32[64,128]{1,0:T(8,128)S(1)} %convert_element_type.60, f32[64,128]{1,0:T(8,128)S(1)} %get-tuple-element.25), kind=kLoop, calls=%fused_computation.21 | loop fusion | flops 13271040 | bytes 37224448 | tf_op jit(solution)/shard_map/add | solution.py:64
  306.8 9.8 %fusion.28 = (f32[324,64,1]{2,0,1:T(8,128)}, f32[324,64,1]{2,0,1:T(8,128)}) fusion(f32[324,64,128]{2,0,1:T(8,128)S(1)} %fusion.15), kind=kLoop, calls=%fused_computation.57 | loop fusion | bytes 331776 | tf_op jit(solution)/shard_map/slice | solution.py:18
  317.3 6.5 copy.19
  323.7 6.5 copy.21
  332.9 15.7 %fusion.29 = (f32[324,63,128]{2,0,1:T(8,128)}, f32[324,63,128]{2,0,1:T(8,128)}) fusion(f32[324,64,128]{2,0,1:T(8,128)} %copy-done), kind=kLoop, calls=%fused_computation.58 | loop fusion | bytes 41803776 | tf_op jit(solution)/shard_map/slice | solution.py:68
  359.8 30.8 %fusion.24 = (bf16[324,64,128]{2,0,1:T(8,128)(2,1)S(1)}, f32[324,64,128]{2,0,1:T(8,128)}) fusion(f32[64,128]{1,0:T(8,128)S(1)} %convert_element_type.60, f32[64,128]{1,0:T(8,128)S(1)} %get-tuple-element.26, f32[324,63,128]{2,0,1:T(8,128)} %get-tuple-element.14, f32[324]{0:T(512)S(1)} %get-tuple-element.31, f32[324,63,128]{2,0,1:T(8,128)} %get-tuple-element.13, ...), kind=kLoop, calls=%fused_computation.54 | loop fusion | flops 37158912 | bytes 47681872 | tf_op jit(solution)/shard_map/convert_element_type | solution.py:54
  390.6 121.2 %all_to_all.41 = bf16[324,64,128]{2,0,1:T(8,128)(2,1)S(1)} all-to-all(bf16[324,64,128]{2,0,1:T(8,128)(2,1)S(1)} %get-tuple-element.5), channel_id=1, replica_groups=mesh['lon'=8,'spec'=4] {'spec'}, dimensions={1} | all-to-all | bytes 10616832 | tf_op jit(solution)/shard_map/all_to_all | solution.py:56
  513.9 9.5 %fusion.19 = bf16[1296,2048]{1,0:T(8,128)(2,1)S(1)} fusion(bf16[1296,1296]{1,0:T(8,128)(2,1)S(1)} %copy-done.3, bf16[162,8,16,128]{3,2,1,0:T(8,128)(2,1)S(1)} %bitcast.103), kind=kOutput, calls=%fused_computation.30 | convolution fusion | flops 6882361344 | bytes 13976064 | tf_op jit(solution)/shard_map/dot_general | solution.py:25
  527.3 118.9 %all_to_all.42 = bf16[4,324,16,128]{3,2,1,0:T(8,128)(2,1)S(1)} all-to-all(bf16[4,324,16,128]{3,2,1,0:T(8,128)(2,1)S(1)} %pad_maximum_fusion.5), channel_id=1, replica_groups=mesh['lon'=8,'spec'=4] {'spec'}, dimensions={0} | all-to-all | bytes 10616832 | tf_op jit(solution)/shard_map/all_to_all | solution.py:59
  652.5 11.3 %copy.25 = f32[324,4,16,128]{3,0,2,1:T(8,128)} copy(f32[324,4,16,128]{3,2,0,1:T(8,128)} %convert_bitcast_fusion) | data formatting | bytes 21233664 | tf_op jit(solution)/shard_map/convert_element_type | solution.py:64
  663.9 8.0 %fusion.14 = f32[324,64,128]{2,0,1:T(8,128)S(1)} fusion(f32[324,64,128]{2,0,1:T(8,128)S(1)} %bitcast.83, f32[324,4,16,128]{3,0,2,1:T(8,128)} %copy.25, bf16[1,324,64,128]{3,2,1,0:T(8,128)(2,1)} %get-tuple-element.15), kind=kLoop, calls=%fused_computation.19 | loop fusion | flops 7962624 | bytes 37158912 | tf_op jit(solution)/shard_map/add | solution.py:64
  671.9 9.4 %fusion.27 = (f32[324,64,1]{2,0,1:T(8,128)}, f32[324,64,1]{2,0,1:T(8,128)}) fusion(f32[324,64,128]{2,0,1:T(8,128)S(1)} %fusion.14), kind=kLoop, calls=%fused_computation.56 | loop fusion | bytes 331776 | tf_op jit(solution)/shard_map/slice | solution.py:18
  682.3 6.5 copy.26
  688.8 6.5 copy.28
  698.0 15.9 %fusion.26 = (f32[324,63,128]{2,0,1:T(8,128)}, f32[324,63,128]{2,0,1:T(8,128)}) fusion(f32[324,64,128]{2,0,1:T(8,128)} %copy-done.1), kind=kLoop, calls=%fused_computation.55 | loop fusion | bytes 41803776 | tf_op jit(solution)/shard_map/slice | solution.py:68
  725.0 29.9 %fusion.3 = f32[324,64,128]{2,0,1:T(8,128)} fusion(f32[324,64,128]{2,0,1:T(8,128)} %copy-done.1, f32[324,64,1]{2,0,1:T(8,128)} %copy.29, f32[324,64,1]{2,0,1:T(8,128)} %copy.27, f32[324,63,128]{2,0,1:T(8,128)} %get-tuple-element.8, f32[324,63,128]{2,0,1:T(8,128)} %get-tuple-element.7, f32[324]{0:T(512)S(1)} %get-tuple-element.31, ...), kind=kLoop, calls=%fused_computation.4 | loop fusion | flops 29196288 | bytes 42307920 | tf_op jit(solution)/shard_map/add | solution.py:41
  755.0 10.2 %copy.30 = f32[324,64,128]{2,1,0:T(8,128)} copy(f32[324,64,128]{2,0,1:T(8,128)} %fusion.3) | data formatting | bytes 21233664 | tf_op jit(solution)/shard_map/add | solution.py:41
  (52 shorter events, 56.4 us)
Async XLA Ops:
  13.1 125.8 %copy-start.2 = (bf16[1296,1296]{1,0:T(8,128)(2,1)S(1)}, bf16[1296,1296]{1,0:T(8,128)(2,1)}, u32[]{:S(2)}) copy-start(bf16[1296,1296]{1,0:T(8,128)(2,1)} %param.10) | copy-start | bytes 10077700
  154.5 121.5 %all-to-all-start.1 = ((bf16[4,324,16,128]{3,2,1,0:T(8,128)(2,1)}), bf16[4,324,16,128]{3,2,1,0:T(8,128)(2,1)}, u32[]{:S(2)}, u32[]{:S(2)}) async-start(bf16[4,324,16,128]{3,2,1,0:T(8,128)(2,1)} %pad_maximum_fusion.4), calls=%async_computation.1 | async-start | bytes 10616832 | tf_op jit(solution)/shard_map/all_to_all | solution.py:59
  306.8 10.5 %copy-start = (f32[324,64,128]{2,0,1:T(8,128)}, f32[324,64,128]{2,0,1:T(8,128)S(1)}, u32[]{:S(2)}) copy-start(f32[324,64,128]{2,0,1:T(8,128)S(1)} %fusion.15) | copy-start | bytes 31850500
  330.2 24.0 %collective-permute-start.1 = (f32[324,64,1]{0,1,2:T(8,128)S(1)}, f32[324,64,1]{0,1,2:T(8,128)S(1)}, u32[]{:S(2)}, u32[]{:S(2)}) collective-permute-start(f32[324,64,1]{0,1,2:T(8,128)S(1)} %copy.21), channel_id=1, source_target_pairs={{0,4},{4,8},{8,12},{12,16},{16,20},{20,24},{24,28},{28,0},{1,5},{5... | collective-permute-start | bytes 248840 | tf_op jit(solution)/shard_map/ppermute | solution.py:15
  330.3 18.4 %collective-permute-start = (f32[324,64,1]{0,1,2:T(8,128)S(1)}, f32[324,64,1]{0,1,2:T(8,128)S(1)}, u32[]{:S(2)}, u32[]{:S(2)}) collective-permute-start(f32[324,64,1]{0,1,2:T(8,128)S(1)} %copy.19), channel_id=1, source_target_pairs={{4,0},{8,4},{12,8},{16,12},{20,16},{24,20},{28,24},{0,28},{5,1},{9... | collective-permute-start | bytes 248840 | tf_op jit(solution)/shard_map/ppermute | solution.py:18
  511.8 2.0 copy-start.3
  646.2 17.6 %slice-start = ((s8[10747904]{0:T(1024)(128)(4,1)}), s8[4194304]{0:T(1024)(128)(4,1)S(1)}, s32[]{:S(2)}) async-start(s8[10747904]{0:T(1024)(128)(4,1)} %bitcast.82), calls=%async_computation.4 | async-start | bytes 8388608
  646.2 17.6 %slice-start.1 = ((s8[10747904]{0:T(1024)(128)(4,1)}), s8[4194304]{0:T(1024)(128)(4,1)S(1)}, s32[]{:S(2)}) async-start(s8[10747904]{0:T(1024)(128)(4,1)} %bitcast.82), calls=%async_computation.5 | async-start | bytes 8388608
  652.5 11.4 %slice-start.2 = ((s8[10747904]{0:T(1024)(128)(4,1)}), s8[2359296]{0:T(1024)(128)(4,1)S(1)}, s32[]{:S(2)}) async-start(s8[10747904]{0:T(1024)(128)(4,1)} %bitcast.82), calls=%async_computation.6 | async-start | bytes 4718592
  671.9 10.4 %copy-start.1 = (f32[324,64,128]{2,0,1:T(8,128)}, f32[324,64,128]{2,0,1:T(8,128)S(1)}, u32[]{:S(2)}) copy-start(f32[324,64,128]{2,0,1:T(8,128)S(1)} %fusion.14) | copy-start | bytes 31850500
  695.3 24.1 %collective-permute-start.3 = (f32[324,64,1]{0,1,2:T(8,128)S(1)}, f32[324,64,1]{0,1,2:T(8,128)S(1)}, u32[]{:S(2)}, u32[]{:S(2)}) collective-permute-start(f32[324,64,1]{0,1,2:T(8,128)S(1)} %copy.28), channel_id=1, source_target_pairs={{0,4},{4,8},{8,12},{12,16},{16,20},{20,24},{24,28},{28,0},{1,5},{5... | collective-permute-start | bytes 248840 | tf_op jit(solution)/shard_map/ppermute | solution.py:15
  695.3 18.5 %collective-permute-start.2 = (f32[324,64,1]{0,1,2:T(8,128)S(1)}, f32[324,64,1]{0,1,2:T(8,128)S(1)}, u32[]{:S(2)}, u32[]{:S(2)}) collective-permute-start(f32[324,64,1]{0,1,2:T(8,128)S(1)} %copy.26), channel_id=1, source_target_pairs={{4,0},{8,4},{12,8},{16,12},{20,16},{24,20},{28,24},{0,28},{5,1},{9... | collective-permute-start | bytes 248840 | tf_op jit(solution)/shard_map/ppermute | solution.py:18
